TPU v7x, 32 devices: a whole 2x2x4 slice. The times are simulated.
32 devices in a mesh: seq: 16 (over z, y, x), head: 2 (over core).
Axes of the slice: x: 2, y: 2, z: 4, core: 2. Of those that a mesh axis runs over, the one named last changes fastest.
Arguments:
- queries: bfloat16 [2048, 2048], P('seq', 'head'), may hold values from -144 to 144
- keys: bfloat16 [2048, 2048], P('seq', 'head'), may hold values from -4 to 4
- values: bfloat16 [2048, 2048], P('seq', 'head'), may hold values from -6 to 6
- grad_out: bfloat16 [2048, 2048], P('seq', 'head'), may hold values from -6 to 6
- bias_table: float32 [32, 128], P('head'), may hold values from -5 to 5
- bucket_ids: int32 [16, 4, 256], P('seq'), may hold values from 0 to 127
- block_mask: int32 [16, 4], P('seq'), may hold values 0 or 1
Outputs:
- grad_queries: bfloat16 [2048, 2048], P('seq', 'head')
- grad_keys: bfloat16 [2048, 2048], P('seq', 'head')
- grad_values: bfloat16 [2048, 2048], P('seq', 'head')
- grad_bias: float32 [32, 128], replicated
All inputs are finite; a program needn't handle non-finite values. No bound on the sum of `block_mask` on one device may be relied on, other than what follows from the above.
Results may differ from a plain program's by a relative error of at most 0.005.
Values may be sent and summed in bfloat16 or wider, within the bound.
No kernel may reach another device: no remote copies, remote signals or barrier semaphores. Data moves between devices by JAX's collectives and lax.ppermute only.
A program may use at most 64 MiB of HBM per device.

v0:
```python
import jax
import jax.numpy as jnp
from jax import lax
from jax.sharding import PartitionSpec as P


def passed_along(value, axis, by):
    devices = lax.axis_size(axis)
    pairs = [(i, i + by) for i in range(devices) if 0 <= i + by < devices]
    return lax.ppermute(value, axis, pairs)


def diagonal_sums(field):
    heads, rows, _ = field.shape
    flipped = field[:, :, ::-1]
    padded = jnp.pad(flipped, ((0, 0), (0, 0), (0, rows)))
    sheared = padded.reshape(heads, 2 * rows * rows)[:, : rows * (2 * rows - 1)]
    sums = sheared.reshape(heads, rows, 2 * rows - 1).sum(axis=1)
    return jnp.pad(sums, ((0, 0), (0, 1)))


def toeplitz_rows(by_offset, rows):
    heads = by_offset.shape[0]
    reverse = by_offset[:, : 2 * rows - 1][:, ::-1]
    tiled = jnp.tile(reverse, (1, rows))
    window = tiled[:, rows - 1 : rows - 1 + rows * (2 * rows - 2)]
    return window.reshape(heads, rows, 2 * rows - 2)[:, :, :rows]


def body(queries, keys, values, grad_out, bias_table, bucket_ids, block_mask):
    tok, width = queries.shape
    heads, buckets = bias_table.shape
    head_dim = width // heads
    span = block_mask.shape[1]
    scale = head_dim ** (-0.5)
    highest = lax.Precision.HIGHEST
    index = lax.axis_index("seq")
    query_heads = queries.reshape(tok, heads, head_dim)
    cot_heads = grad_out.reshape(tok, heads, head_dim)
    rows = jnp.arange(tok, dtype=jnp.int32)
    lower = rows[:, None] >= rows[None, :]
    codes = jnp.arange(buckets, dtype=jnp.int32)
    table_ids = bucket_ids[0]
    flags = block_mask[0]

    def pair_terms(key_blk, value_blk, step):
        ids = lax.dynamic_index_in_dim(table_ids, step, 0, keepdims=False)
        onehot = (ids[:, None] == codes[None, :]).astype(jnp.float32)
        by_offset = jnp.dot(bias_table, onehot.T, precision=highest)
        bias_full = toeplitz_rows(by_offset, tok)
        key_heads = key_blk.reshape(tok, heads, head_dim)
        value_heads = value_blk.reshape(tok, heads, head_dim)
        scores = (
            scale
            * jnp.einsum("qhd,khd->hqk", query_heads, key_heads, preferred_element_type=jnp.float32)
            + bias_full
        )
        dprob = jnp.einsum(
            "qhd,khd->hqk", cot_heads, value_heads, preferred_element_type=jnp.float32
        )
        flag = lax.dynamic_index_in_dim(flags, step, 0, keepdims=False)
        whole = (flag == 1) & (index - step >= 0)
        valid = jnp.where(step == 0, lower, whole)
        masked = jnp.where(valid[None], scores, jnp.float32(-1e30))
        return (onehot, key_heads, masked, valid, dprob)

    def forward_step(stats, key_blk, value_blk, step):
        most, total, accum = stats
        _, _, masked, valid, dprob = pair_terms(key_blk, value_blk, step)
        top = jnp.maximum(most, masked.max(axis=-1))
        weights = jnp.where(valid[None], jnp.exp(masked - top[..., None]), jnp.float32(0.0))
        factor = jnp.exp(most - top)
        return (
            top,
            total * factor + weights.sum(axis=-1),
            accum * factor + (weights * dprob).sum(axis=-1),
        )

    zeros_rows = jnp.zeros((heads, tok), jnp.float32)
    stats = forward_step(
        (jnp.full((heads, tok), -1e30, jnp.float32), zeros_rows, zeros_rows), keys, values, 0
    )
    stash = (
        jnp.zeros((span, tok, width), keys.dtype).at[0].set(keys),
        jnp.zeros((span, tok, width), values.dtype).at[0].set(values),
    )

    def forward_loop(step, carry):
        key_blk, value_blk, stats, stash = carry
        key_blk, value_blk = passed_along((key_blk, value_blk), "seq", 1)
        stats = forward_step(stats, key_blk, value_blk, step)
        stash = (
            lax.dynamic_update_index_in_dim(stash[0], key_blk, step, 0),
            lax.dynamic_update_index_in_dim(stash[1], value_blk, step, 0),
        )
        return (key_blk, value_blk, stats, stash)

    _, _, stats, stash = lax.fori_loop(1, span, forward_loop, (keys, values, stats, stash))
    most, total, accum = stats
    lse = most + jnp.log(total)
    delta = accum / total

    def backward_terms(key_blk, value_blk, step):
        onehot, key_heads, masked, valid, dprob = pair_terms(key_blk, value_blk, step)
        prob = jnp.exp(masked - lse[..., None])
        dscore = prob * (dprob - delta[..., None])
        score16 = dscore.astype(jnp.bfloat16)
        prob16 = prob.astype(jnp.bfloat16)
        grad_q = scale * jnp.einsum(
            "hqk,khd->qhd", score16, key_heads, preferred_element_type=jnp.float32
        ).reshape(tok, width)
        grad_k = scale * jnp.einsum(
            "hqk,qhd->khd", score16, query_heads, preferred_element_type=jnp.float32
        ).reshape(tok, width)
        grad_v = jnp.einsum(
            "hqk,qhd->khd", prob16, cot_heads, preferred_element_type=jnp.float32
        ).reshape(tok, width)
        grad_b = jnp.dot(diagonal_sums(dscore), onehot, precision=highest)
        return (grad_q, grad_k, grad_v, grad_b)

    last = span - 1
    first_terms = backward_terms(stash[0][last], stash[1][last], last)

    def chain_loop(turn, carry):
        grad_q, grad_k, grad_v, grad_b = carry
        step = span - 2 - turn
        grad_k, grad_v = passed_along((grad_k, grad_v), "seq", -1)
        key_blk = lax.dynamic_index_in_dim(stash[0], step, 0, keepdims=False)
        value_blk = lax.dynamic_index_in_dim(stash[1], step, 0, keepdims=False)
        more = backward_terms(key_blk, value_blk, step)
        return (grad_q + more[0], grad_k + more[1], grad_v + more[2], grad_b + more[3])

    grad_q, grad_k, grad_v, grad_b = lax.fori_loop(0, span - 1, chain_loop, first_terms)
    key_grad = grad_k.astype(jnp.bfloat16)
    value_grad = grad_v.astype(jnp.bfloat16)
    summed = lax.psum(grad_b, "seq")
    grad_bias = lax.all_gather(summed, "head", axis=0, tiled=True)
    return (grad_q.astype(jnp.bfloat16), key_grad, value_grad, grad_bias)


def solution(mesh):
    placed = (
        P("seq", "head"),
        P("seq", "head"),
        P("seq", "head"),
        P("seq", "head"),
        P("head", None),
        P("seq", None, None),
        P("seq", None),
    )
    return jax.shard_map(
        body,
        mesh=mesh,
        in_specs=placed,
        out_specs=(P("seq", "head"), P("seq", "head"), P("seq", "head"), P()),
        check_vma=False,
    )
```

profile of v0, /device:TPU:0, one launch (start us, length us, event | category | flops | bytes accessed | tf_op | source)
XLA Modules:
  0.0 294.3 jit_solution(14736967456666874631)
XLA Ops:
  5.7 2.5 tile.67
  10.3 4.5 %reshape.290 = f32[16,128,254]{2,1,0:T(8,128)} reshape(f32[16,32512]{1,0:T(8,128)S(1)} %slice.162) | data formatting | bytes 4161536 | tf_op jit(solution)/shard_map/reshape | solution.py:27
  23.1 72.6 %while.52 = (s32[]{:T(128)}, bf16[128,1024]{0,1:T(8,128)(2,1)S(1)}, bf16[128,1024]{0,1:T(8,128)(2,1)}, f32[16,128]{1,0:T(8,128)S(1)}, f32[16,128]{1,0:T(8,128)S(...) while((s32[]{:T(128)}, bf16[128,1024]{0,1:T(8,128)(2,1)S(1)}, ...), condition=%wide.region_7.8_spmd.clone, body=%wide.region_3.7_spmd.clone.sunk | while | flops 76355592 | bytes 29592764 | solution.py:98
  23.1 4.9 %collective-permute-start = (bf16[128,1024]{0,1:T(8,128)(2,1)S(1)}, bf16[128,1024]{0,1:T(8,128)(2,1)S(1)}, u32[]{:S(2)}, u32[]{:S(2)}) collective-permute-start(bf16[128,1024]{0,1:T(8,128)(2,1)S(1)} %get-tuple-element.1186), channel_id=1, source_target_pairs={{0,2},{2,4},{4,6},{6,8},{8,10},{10,12},{12,14},{14,16},{16,18},{18... | collective-permute-start | bytes 786440 | tf_op jit(solution)/shard_map/while/body/eval_jaxpr/ppermute | solution.py:10
  28.0 3.4 %collective-permute-start.1 = (bf16[128,1024]{0,1:T(8,128)(2,1)}, bf16[128,1024]{0,1:T(8,128)(2,1)S(1)}, u32[]{:S(2)}, u32[]{:S(2)}) collective-permute-start(bf16[128,1024]{0,1:T(8,128)(2,1)} %get-tuple-element.1187), channel_id=1, source_target_pairs={{0,2},{2,4},{4,6},{6,8},{8,10},{10,12},{12,14},{14,16},{16,18},{18... | collective-permute-start | bytes 786440 | tf_op jit(solution)/shard_map/while/body/eval_jaxpr/ppermute | solution.py:10
  32.1 2.5 tile.79
  36.8 4.5 %reshape.311 = f32[16,128,254]{2,1,0:T(8,128)} reshape(f32[16,32512]{1,0:T(8,128)S(1)} %slice.180) | data formatting | bytes 4161536 | tf_op jit(solution)/shard_map/while/body/eval_jaxpr/reshape | solution.py:27
  48.3 3.4 %collective-permute-start = (bf16[128,1024]{0,1:T(8,128)(2,1)S(1)}, bf16[128,1024]{0,1:T(8,128)(2,1)S(1)}, u32[]{:S(2)}, u32[]{:S(2)}) collective-permute-start(bf16[128,1024]{0,1:T(8,128)(2,1)S(1)} %get-tuple-element.1186), channel_id=1, source_target_pairs={{0,2},{2,4},{4,6},{6,8},{8,10},{10,12},{12,14},{14,16},{16,18},{18... | collective-permute-start | bytes 786440 | tf_op jit(solution)/shard_map/while/body/eval_jaxpr/ppermute | solution.py:10
  51.7 3.4 %collective-permute-start.1 = (bf16[128,1024]{0,1:T(8,128)(2,1)}, bf16[128,1024]{0,1:T(8,128)(2,1)S(1)}, u32[]{:S(2)}, u32[]{:S(2)}) collective-permute-start(bf16[128,1024]{0,1:T(8,128)(2,1)} %get-tuple-element.1187), channel_id=1, source_target_pairs={{0,2},{2,4},{4,6},{6,8},{8,10},{10,12},{12,14},{14,16},{16,18},{18... | collective-permute-start | bytes 786440 | tf_op jit(solution)/shard_map/while/body/eval_jaxpr/ppermute | solution.py:10
  55.8 2.5 tile.79
  60.5 4.5 %reshape.311 = f32[16,128,254]{2,1,0:T(8,128)} reshape(f32[16,32512]{1,0:T(8,128)S(1)} %slice.180) | data formatting | bytes 4161536 | tf_op jit(solution)/shard_map/while/body/eval_jaxpr/reshape | solution.py:27
  72.0 3.4 %collective-permute-start = (bf16[128,1024]{0,1:T(8,128)(2,1)S(1)}, bf16[128,1024]{0,1:T(8,128)(2,1)S(1)}, u32[]{:S(2)}, u32[]{:S(2)}) collective-permute-start(bf16[128,1024]{0,1:T(8,128)(2,1)S(1)} %get-tuple-element.1186), channel_id=1, source_target_pairs={{0,2},{2,4},{4,6},{6,8},{8,10},{10,12},{12,14},{14,16},{16,18},{18... | collective-permute-start | bytes 786440 | tf_op jit(solution)/shard_map/while/body/eval_jaxpr/ppermute | solution.py:10
  75.4 3.4 %collective-permute-start.1 = (bf16[128,1024]{0,1:T(8,128)(2,1)}, bf16[128,1024]{0,1:T(8,128)(2,1)S(1)}, u32[]{:S(2)}, u32[]{:S(2)}) collective-permute-start(bf16[128,1024]{0,1:T(8,128)(2,1)} %get-tuple-element.1187), channel_id=1, source_target_pairs={{0,2},{2,4},{4,6},{6,8},{8,10},{10,12},{12,14},{14,16},{16,18},{18... | collective-permute-start | bytes 786440 | tf_op jit(solution)/shard_map/while/body/eval_jaxpr/ppermute | solution.py:10
  84.2 4.5 %reshape.311 = f32[16,128,254]{2,1,0:T(8,128)} reshape(f32[16,32512]{1,0:T(8,128)S(1)} %slice.180) | data formatting | bytes 4161536 | tf_op jit(solution)/shard_map/while/body/eval_jaxpr/reshape | solution.py:27
  102.8 4.5 %reshape.295 = f32[16,128,254]{2,1,0:T(8,128)} reshape(f32[16,32512]{1,0:T(8,128)S(1)} %slice.165) | data formatting | bytes 4161536 | tf_op jit(solution)/shard_map/reshape | solution.py:27
  122.1 4.8 %reshape.298 = f32[16,128,255]{2,1,0:T(8,128)S(1)} reshape(f32[16,32640]{1,0:T(8,128)} %slice.167) | data formatting | bytes 4177920 | tf_op jit(solution)/shard_map/reshape | solution.py:18
  127.3 105.1 %while.53 = (s32[]{:T(128)}, f32[128,1024]{0,1:T(8,128)}, f32[128,1024]{0,1:T(8,128)}, f32[128,1024]{0,1:T(8,128)}, f32[16,128]{1,0:T(8,128)S(1)}, /*index=5*/bf...) while((s32[]{:T(128)}, f32[128,1024]{0,1:T(8,128)}, ...), condition=%wide.region_11.12_spmd.clone, body=%wide.region_9.11_spmd.clone.sunk | while | flops 183988240 | bytes 71119040 | solution.py:133
  135.4 4.5 %reshape.312 = f32[16,128,254]{2,1,0:T(8,128)} reshape(f32[16,32512]{1,0:T(8,128)S(1)} %slice.183) | data formatting | bytes 4161536 | tf_op jit(solution)/shard_map/while/body/eval_jaxpr/reshape | solution.py:27
  151.6 4.8 %reshape.313 = f32[16,128,255]{2,1,0:T(8,128)S(1)} reshape(f32[16,32640]{1,0:T(8,128)} %slice.185) | data formatting | bytes 4177920 | tf_op jit(solution)/shard_map/while/body/eval_jaxpr/reshape | solution.py:18
  170.4 4.5 %reshape.312 = f32[16,128,254]{2,1,0:T(8,128)} reshape(f32[16,32512]{1,0:T(8,128)S(1)} %slice.183) | data formatting | bytes 4161536 | tf_op jit(solution)/shard_map/while/body/eval_jaxpr/reshape | solution.py:27
  186.5 4.8 %reshape.313 = f32[16,128,255]{2,1,0:T(8,128)S(1)} reshape(f32[16,32640]{1,0:T(8,128)} %slice.185) | data formatting | bytes 4177920 | tf_op jit(solution)/shard_map/while/body/eval_jaxpr/reshape | solution.py:18
  205.4 4.5 %reshape.312 = f32[16,128,254]{2,1,0:T(8,128)} reshape(f32[16,32512]{1,0:T(8,128)S(1)} %slice.183) | data formatting | bytes 4161536 | tf_op jit(solution)/shard_map/while/body/eval_jaxpr/reshape | solution.py:27
  221.5 4.8 %reshape.313 = f32[16,128,255]{2,1,0:T(8,128)S(1)} reshape(f32[16,32640]{1,0:T(8,128)} %slice.185) | data formatting | bytes 4177920 | tf_op jit(solution)/shard_map/while/body/eval_jaxpr/reshape | solution.py:18
  238.0 53.8 %psum.7 = f32[16,128]{1,0:T(8,128)S(1)} all-reduce(f32[16,128]{1,0:T(8,128)S(1)} %get-tuple-element.814), channel_id=1, replica_groups=mesh['seq'=16,'head'=2] {'seq'}, use_global_device_ids=true, to_apply=%region_12.13 | all-reduce | flops 2048 | bytes 16384 | tf_op jit(solution)/shard_map/psum | solution.py:136
  (253 shorter events, 149.1 us)
Async XLA Ops:
  19.7 3.4 %copy-start.7 = (s32[1,4,256]{2,1,0:T(4,128)S(1)}, s32[1,4,256]{2,1,0:T(4,128)}, u32[]{:S(2)}) copy-start(s32[1,4,256]{2,1,0:T(4,128)} %param.20) | copy-start | bytes 12292
  19.7 3.4 %copy-start.8 = (f32[16,128]{1,0:T(8,128)S(1)}, f32[16,128]{1,0:T(8,128)}, u32[]{:S(2)}) copy-start(f32[16,128]{1,0:T(8,128)} %param.19) | copy-start | bytes 24580
  19.7 3.4 %copy-start.9 = (s32[1,4]{1,0:T(1,128)S(1)}, s32[1,4]{1,0:T(1,128)}, u32[]{:S(2)}) copy-start(s32[1,4]{1,0:T(1,128)} %param.21) | copy-start | bytes 52
  23.1 21.0 %collective-permute-start = (bf16[128,1024]{0,1:T(8,128)(2,1)S(1)}, bf16[128,1024]{0,1:T(8,128)(2,1)S(1)}, u32[]{:S(2)}, u32[]{:S(2)}) collective-permute-start(bf16[128,1024]{0,1:T(8,128)(2,1)S(1)} %get-tuple-element.1186), channel_id=1, source_target_pairs={{0,2},{2,4},{4,6},{6,8},{8,10},{10,12},{12,14},{14,16},{16,18},{18... | collective-permute-start | bytes 786440 | tf_op jit(solution)/shard_map/while/body/eval_jaxpr/ppermute | solution.py:10
  28.0 16.7 %collective-permute-start.1 = (bf16[128,1024]{0,1:T(8,128)(2,1)}, bf16[128,1024]{0,1:T(8,128)(2,1)S(1)}, u32[]{:S(2)}, u32[]{:S(2)}) collective-permute-start(bf16[128,1024]{0,1:T(8,128)(2,1)} %get-tuple-element.1187), channel_id=1, source_target_pairs={{0,2},{2,4},{4,6},{6,8},{8,10},{10,12},{12,14},{14,16},{16,18},{18... | collective-permute-start | bytes 786440 | tf_op jit(solution)/shard_map/while/body/eval_jaxpr/ppermute | solution.py:10
  48.3 19.5 %collective-permute-start = (bf16[128,1024]{0,1:T(8,128)(2,1)S(1)}, bf16[128,1024]{0,1:T(8,128)(2,1)S(1)}, u32[]{:S(2)}, u32[]{:S(2)}) collective-permute-start(bf16[128,1024]{0,1:T(8,128)(2,1)S(1)} %get-tuple-element.1186), channel_id=1, source_target_pairs={{0,2},{2,4},{4,6},{6,8},{8,10},{10,12},{12,14},{14,16},{16,18},{18... | collective-permute-start | bytes 786440 | tf_op jit(solution)/shard_map/while/body/eval_jaxpr/ppermute | solution.py:10
  51.7 16.7 %collective-permute-start.1 = (bf16[128,1024]{0,1:T(8,128)(2,1)}, bf16[128,1024]{0,1:T(8,128)(2,1)S(1)}, u32[]{:S(2)}, u32[]{:S(2)}) collective-permute-start(bf16[128,1024]{0,1:T(8,128)(2,1)} %get-tuple-element.1187), channel_id=1, source_target_pairs={{0,2},{2,4},{4,6},{6,8},{8,10},{10,12},{12,14},{14,16},{16,18},{18... | collective-permute-start | bytes 786440 | tf_op jit(solution)/shard_map/while/body/eval_jaxpr/ppermute | solution.py:10
  72.0 19.5 %collective-permute-start = (bf16[128,1024]{0,1:T(8,128)(2,1)S(1)}, bf16[128,1024]{0,1:T(8,128)(2,1)S(1)}, u32[]{:S(2)}, u32[]{:S(2)}) collective-permute-start(bf16[128,1024]{0,1:T(8,128)(2,1)S(1)} %get-tuple-element.1186), channel_id=1, source_target_pairs={{0,2},{2,4},{4,6},{6,8},{8,10},{10,12},{12,14},{14,16},{16,18},{18... | collective-permute-start | bytes 786440 | tf_op jit(solution)/shard_map/while/body/eval_jaxpr/ppermute | solution.py:10
  75.4 16.7 %collective-permute-start.1 = (bf16[128,1024]{0,1:T(8,128)(2,1)}, bf16[128,1024]{0,1:T(8,128)(2,1)S(1)}, u32[]{:S(2)}, u32[]{:S(2)}) collective-permute-start(bf16[128,1024]{0,1:T(8,128)(2,1)} %get-tuple-element.1187), channel_id=1, source_target_pairs={{0,2},{2,4},{4,6},{6,8},{8,10},{10,12},{12,14},{14,16},{16,18},{18... | collective-permute-start | bytes 786440 | tf_op jit(solution)/shard_map/while/body/eval_jaxpr/ppermute | solution.py:10
  111.6 2.3 copy-start.4
  127.5 31.0 %collective-permute-start.2 = (f32[128,1024]{0,1:T(8,128)}, f32[128,1024]{0,1:T(8,128)}, u32[]{:S(2)}, u32[]{:S(2)}) collective-permute-start(f32[128,1024]{0,1:T(8,128)} %get-tuple-element.1244), channel_id=1, source_target_pairs={{2,0},{4,2},{6,4},{8,6},{10,8},{12,10},{14,12},{16,14},{18,16},{20... | collective-permute-start | bytes 1572872 | tf_op jit(solution)/shard_map/while/body/eval_jaxpr/ppermute | solution.py:10
  128.8 31.8 %collective-permute-start.3 = (f32[128,1024]{0,1:T(8,128)}, f32[128,1024]{0,1:T(8,128)}, u32[]{:S(2)}, u32[]{:S(2)}) collective-permute-start(f32[128,1024]{0,1:T(8,128)} %get-tuple-element.1245), channel_id=1, source_target_pairs={{2,0},{4,2},{6,4},{8,6},{10,8},{12,10},{14,12},{16,14},{18,16},{20... | collective-permute-start | bytes 1572872 | tf_op jit(solution)/shard_map/while/body/eval_jaxpr/ppermute | solution.py:10
  156.6 1.8 copy-start.2
  156.6 1.9 copy-start
  158.5 4.0 %copy-start.3 = (f32[128,1024]{0,1:T(8,128)}, f32[128,1024]{0,1:T(8,128)S(1)}, u32[]{:S(2)}) copy-start(f32[128,1024]{0,1:T(8,128)S(1)} %bitcast_add_fusion.6) | copy-start | bytes 1572868 | tf_op jit(solution)/shard_map/while
  162.5 31.0 %collective-permute-start.2 = (f32[128,1024]{0,1:T(8,128)}, f32[128,1024]{0,1:T(8,128)}, u32[]{:S(2)}, u32[]{:S(2)}) collective-permute-start(f32[128,1024]{0,1:T(8,128)} %get-tuple-element.1244), channel_id=1, source_target_pairs={{2,0},{4,2},{6,4},{8,6},{10,8},{12,10},{14,12},{16,14},{18,16},{20... | collective-permute-start | bytes 1572872 | tf_op jit(solution)/shard_map/while/body/eval_jaxpr/ppermute | solution.py:10
  163.7 31.8 %collective-permute-start.3 = (f32[128,1024]{0,1:T(8,128)}, f32[128,1024]{0,1:T(8,128)}, u32[]{:S(2)}, u32[]{:S(2)}) collective-permute-start(f32[128,1024]{0,1:T(8,128)} %get-tuple-element.1245), channel_id=1, source_target_pairs={{2,0},{4,2},{6,4},{8,6},{10,8},{12,10},{14,12},{16,14},{18,16},{20... | collective-permute-start | bytes 1572872 | tf_op jit(solution)/shard_map/while/body/eval_jaxpr/ppermute | solution.py:10
  191.5 1.9 copy-start
  193.4 4.0 %copy-start.3 = (f32[128,1024]{0,1:T(8,128)}, f32[128,1024]{0,1:T(8,128)S(1)}, u32[]{:S(2)}) copy-start(f32[128,1024]{0,1:T(8,128)S(1)} %bitcast_add_fusion.6) | copy-start | bytes 1572868 | tf_op jit(solution)/shard_map/while
  197.4 31.0 %collective-permute-start.2 = (f32[128,1024]{0,1:T(8,128)}, f32[128,1024]{0,1:T(8,128)}, u32[]{:S(2)}, u32[]{:S(2)}) collective-permute-start(f32[128,1024]{0,1:T(8,128)} %get-tuple-element.1244), channel_id=1, source_target_pairs={{2,0},{4,2},{6,4},{8,6},{10,8},{12,10},{14,12},{16,14},{18,16},{20... | collective-permute-start | bytes 1572872 | tf_op jit(solution)/shard_map/while/body/eval_jaxpr/ppermute | solution.py:10
  198.7 31.8 %collective-permute-start.3 = (f32[128,1024]{0,1:T(8,128)}, f32[128,1024]{0,1:T(8,128)}, u32[]{:S(2)}, u32[]{:S(2)}) collective-permute-start(f32[128,1024]{0,1:T(8,128)} %get-tuple-element.1245), channel_id=1, source_target_pairs={{2,0},{4,2},{6,4},{8,6},{10,8},{12,10},{14,12},{16,14},{18,16},{20... | collective-permute-start | bytes 1572872 | tf_op jit(solution)/shard_map/while/body/eval_jaxpr/ppermute | solution.py:10
  226.5 1.8 copy-start.2
  226.5 1.9 copy-start
  228.4 4.0 %copy-start.3 = (f32[128,1024]{0,1:T(8,128)}, f32[128,1024]{0,1:T(8,128)S(1)}, u32[]{:S(2)}) copy-start(f32[128,1024]{0,1:T(8,128)S(1)} %bitcast_add_fusion.6) | copy-start | bytes 1572868 | tf_op jit(solution)/shard_map/while
  (14 other events, 19.5 us)
where the time goes:
time: 297 us; the launch traced here: 294 us
  local copies, waits for them, and re-layouts  154 us (52%)
  blocking collectives  55.6 us (19%)
  matrix products  34.3 us (12%)
  starting transfers between devices  29.6 us (10%)
  other arithmetic  13.8 us (5%)
  loops' own time  5.03 us (2%)
    psum x1, blocking collectives, body(): summed = lax.psum(grad_b, 'seq')  53.8 us
    reshape x8, local copies, waits for them, and re-layouts, toeplitz_rows(): return window.reshape(heads, rows, 2 * rows - 2)[:, :, :rows]  36.3 us
    ppermute x12, starting transfers between devices, passed_along(): return lax.ppermute(value, axis, pairs)  29.6 us
    another operation x16, local copies, waits for them, and re-layouts, toeplitz_rows(): tiled = jnp.tile(reverse, (1, rows))  21.1 us
    reshape x4, local copies, waits for them, and re-layouts, diagonal_sums(): sums = sheared.reshape(heads, rows, 2 * rows - 1).sum(axis=1)  19.2 us
    slice x8, local copies, waits for them, and re-layouts, toeplitz_rows(): window = tiled[:, rows - 1:rows - 1 + rows * (2 * rows - 2)]  17.5 us
    dot_general x8, matrix products, pair_terms(): jnp.einsum('qhd,khd->hqk', cot_heads, value_heads, preferred_element_type...  10.8 us
    while x57, local copies, waits for them, and re-layouts  10.6 us
  transfers between devices with their start and end apart: 12, of which 0 were waited for; matrix products, arithmetic and copies ran while one was open for 41% of the time, Pallas kernels for 0%

commit v1 on v0

--- a/solution.py
+++ b/solution.py
@@ -133,7 +133,11 @@
     grad_q, grad_k, grad_v, grad_b = lax.fori_loop(0, span - 1, chain_loop, first_terms)
     key_grad = grad_k.astype(jnp.bfloat16)
     value_grad = grad_v.astype(jnp.bfloat16)
-    summed = lax.psum(grad_b, "seq")
+    size = lax.axis_size("seq")
+    summed, reach = (grad_b, 1)
+    while reach < size:
+        summed = summed + lax.ppermute(summed, "seq", [(i_2, i_2 ^ reach) for i_2 in range(size)])
+        reach = 2 * reach
     grad_bias = lax.all_gather(summed, "head", axis=0, tiled=True)
     return (grad_q.astype(jnp.bfloat16), key_grad, value_grad, grad_bias)
 

time: 297 us -> 269 us (0.906)
  blocking collectives: 55.6 us -> 1.81 us
  starting transfers between devices: 29.6 us -> 49.6 us
  waiting for transfers between devices: 0.03 us -> 4.92 us
    psum x1 -> x0, blocking collectives: 53.8 us -> none  [body(): summed = lax.psum(grad_b, 'seq')]
    ppermute x0 -> x4, starting transfers between devices: none -> 20.1 us  [body(): lax.ppermute(summed, 'seq', [(i_2, i_2 ^ reach) for i_2 in range(size)])]
    ppermute x0 -> x4, waiting for transfers between devices: none -> 4.89 us  [body(): lax.ppermute(summed, 'seq', [(i_2, i_2 ^ reach) for i_2 in range(size)])]
    unnamed x25 -> x27, local copies, waits for them, and re-layouts: 7.77 us -> 7.78 us
  transfers between devices with their start and end apart: 12 -> 16, of which waited for: 0 -> 3; matrix products, arithmetic and copies ran while one was open for 41% -> 47% of each run, Pallas kernels for 0% -> 0%
where the time goes in v1:
time: 269 us; the launch traced here: 266 us
  local copies, waits for them, and re-layouts  155 us (58%)
  starting transfers between devices  49.6 us (18%)
  matrix products  34.4 us (13%)
  other arithmetic  13.7 us (5%)
  loops' own time  5.07 us (2%)
  waiting for transfers between devices  4.92 us (2%)
    reshape x8, local copies, waits for them, and re-layouts, toeplitz_rows(): return window.reshape(heads, rows, 2 * rows - 2)[:, :, :rows]  36.4 us
    ppermute x12, starting transfers between devices, passed_along(): return lax.ppermute(value, axis, pairs)  29.6 us
    another operation x16, local copies, waits for them, and re-layouts, toeplitz_rows(): tiled = jnp.tile(reverse, (1, rows))  21.1 us
    ppermute x4, starting transfers between devices, body(): lax.ppermute(summed, 'seq', [(i_2, i_2 ^ reach) for i_2 in range(size)])  20.1 us
    reshape x4, local copies, waits for them, and re-layouts, diagonal_sums(): sums = sheared.reshape(heads, rows, 2 * rows - 1).sum(axis=1)  19.2 us
    slice x8, local copies, waits for them, and re-layouts, toeplitz_rows(): window = tiled[:, rows - 1:rows - 1 + rows * (2 * rows - 2)]  17.5 us
    dot_general x8, matrix products, pair_terms(): jnp.einsum('qhd,khd->hqk', cot_heads, value_heads, preferred_element_type...  10.8 us
    while x57, local copies, waits for them, and re-layouts  10.6 us
  transfers between devices with their start and end apart: 16, of which 3 were waited for; matrix products, arithmetic and copies ran while one was open for 47% of the time, Pallas kernels for 0%

profile of v1, /device:TPU:0, one launch (start us, length us, event | category | flops | bytes accessed | tf_op | source)
XLA Modules:
  0.0 266.4 jit_solution(17154243849417206901)
XLA Ops:
  10.3 4.5 %reshape.290 = f32[16,128,254]{2,1,0:T(8,128)} reshape(f32[16,32512]{1,0:T(8,128)S(1)} %slice.162) | data formatting | bytes 4161536 | tf_op jit(solution)/shard_map/reshape | solution.py:27
  23.8 72.8 %while.52 = (s32[]{:T(128)}, bf16[128,1024]{0,1:T(8,128)(2,1)S(1)}, bf16[128,1024]{0,1:T(8,128)(2,1)}, f32[16,128]{1,0:T(8,128)S(1)}, f32[16,128]{1,0:T(8,128)S(...) while((s32[]{:T(128)}, bf16[128,1024]{0,1:T(8,128)(2,1)S(1)}, ...), condition=%wide.region_7.8_spmd.clone, body=%wide.region_3.7_spmd.clone.sunk | while | flops 76355592 | bytes 29592764 | solution.py:98
  23.8 4.9 %collective-permute-start = (bf16[128,1024]{0,1:T(8,128)(2,1)S(1)}, bf16[128,1024]{0,1:T(8,128)(2,1)S(1)}, u32[]{:S(2)}, u32[]{:S(2)}) collective-permute-start(bf16[128,1024]{0,1:T(8,128)(2,1)S(1)} %get-tuple-element.1186), channel_id=1, source_target_pairs={{0,2},{2,4},{4,6},{6,8},{8,10},{10,12},{12,14},{14,16},{16,18},{18... | collective-permute-start | bytes 786440 | tf_op jit(solution)/shard_map/while/body/eval_jaxpr/ppermute | solution.py:10
  28.7 3.4 %collective-permute-start.1 = (bf16[128,1024]{0,1:T(8,128)(2,1)}, bf16[128,1024]{0,1:T(8,128)(2,1)S(1)}, u32[]{:S(2)}, u32[]{:S(2)}) collective-permute-start(bf16[128,1024]{0,1:T(8,128)(2,1)} %get-tuple-element.1187), channel_id=1, source_target_pairs={{0,2},{2,4},{4,6},{6,8},{8,10},{10,12},{12,14},{14,16},{16,18},{18... | collective-permute-start | bytes 786440 | tf_op jit(solution)/shard_map/while/body/eval_jaxpr/ppermute | solution.py:10
  37.5 4.5 %reshape.311 = f32[16,128,254]{2,1,0:T(8,128)} reshape(f32[16,32512]{1,0:T(8,128)S(1)} %slice.180) | data formatting | bytes 4161536 | tf_op jit(solution)/shard_map/while/body/eval_jaxpr/reshape | solution.py:27
  49.1 3.4 %collective-permute-start = (bf16[128,1024]{0,1:T(8,128)(2,1)S(1)}, bf16[128,1024]{0,1:T(8,128)(2,1)S(1)}, u32[]{:S(2)}, u32[]{:S(2)}) collective-permute-start(bf16[128,1024]{0,1:T(8,128)(2,1)S(1)} %get-tuple-element.1186), channel_id=1, source_target_pairs={{0,2},{2,4},{4,6},{6,8},{8,10},{10,12},{12,14},{14,16},{16,18},{18... | collective-permute-start | bytes 786440 | tf_op jit(solution)/shard_map/while/body/eval_jaxpr/ppermute | solution.py:10
  52.5 3.4 %collective-permute-start.1 = (bf16[128,1024]{0,1:T(8,128)(2,1)}, bf16[128,1024]{0,1:T(8,128)(2,1)S(1)}, u32[]{:S(2)}, u32[]{:S(2)}) collective-permute-start(bf16[128,1024]{0,1:T(8,128)(2,1)} %get-tuple-element.1187), channel_id=1, source_target_pairs={{0,2},{2,4},{4,6},{6,8},{8,10},{10,12},{12,14},{14,16},{16,18},{18... | collective-permute-start | bytes 786440 | tf_op jit(solution)/shard_map/while/body/eval_jaxpr/ppermute | solution.py:10
  61.2 4.5 %reshape.311 = f32[16,128,254]{2,1,0:T(8,128)} reshape(f32[16,32512]{1,0:T(8,128)S(1)} %slice.180) | data formatting | bytes 4161536 | tf_op jit(solution)/shard_map/while/body/eval_jaxpr/reshape | solution.py:27
  72.8 3.4 %collective-permute-start = (bf16[128,1024]{0,1:T(8,128)(2,1)S(1)}, bf16[128,1024]{0,1:T(8,128)(2,1)S(1)}, u32[]{:S(2)}, u32[]{:S(2)}) collective-permute-start(bf16[128,1024]{0,1:T(8,128)(2,1)S(1)} %get-tuple-element.1186), channel_id=1, source_target_pairs={{0,2},{2,4},{4,6},{6,8},{8,10},{10,12},{12,14},{14,16},{16,18},{18... | collective-permute-start | bytes 786440 | tf_op jit(solution)/shard_map/while/body/eval_jaxpr/ppermute | solution.py:10
  76.2 3.4 %collective-permute-start.1 = (bf16[128,1024]{0,1:T(8,128)(2,1)}, bf16[128,1024]{0,1:T(8,128)(2,1)S(1)}, u32[]{:S(2)}, u32[]{:S(2)}) collective-permute-start(bf16[128,1024]{0,1:T(8,128)(2,1)} %get-tuple-element.1187), channel_id=1, source_target_pairs={{0,2},{2,4},{4,6},{6,8},{8,10},{10,12},{12,14},{14,16},{16,18},{18... | collective-permute-start | bytes 786440 | tf_op jit(solution)/shard_map/while/body/eval_jaxpr/ppermute | solution.py:10
  85.0 4.5 %reshape.311 = f32[16,128,254]{2,1,0:T(8,128)} reshape(f32[16,32512]{1,0:T(8,128)S(1)} %slice.180) | data formatting | bytes 4161536 | tf_op jit(solution)/shard_map/while/body/eval_jaxpr/reshape | solution.py:27
  103.6 4.5 %reshape.295 = f32[16,128,254]{2,1,0:T(8,128)} reshape(f32[16,32512]{1,0:T(8,128)S(1)} %slice.165) | data formatting | bytes 4161536 | tf_op jit(solution)/shard_map/reshape | solution.py:27
  123.2 4.8 %reshape.298 = f32[16,128,255]{2,1,0:T(8,128)S(1)} reshape(f32[16,32640]{1,0:T(8,128)} %slice.167) | data formatting | bytes 4177920 | tf_op jit(solution)/shard_map/reshape | solution.py:18
  128.4 105.0 %while.53 = (s32[]{:T(128)}, f32[128,1024]{0,1:T(8,128)}, f32[128,1024]{0,1:T(8,128)}, f32[128,1024]{0,1:T(8,128)}, f32[16,128]{1,0:T(8,128)S(1)}, /*index=5*/bf...) while((s32[]{:T(128)}, f32[128,1024]{0,1:T(8,128)}, ...), condition=%wide.region_11.12_spmd.clone, body=%wide.region_9.11_spmd.clone.sunk | while | flops 183988240 | bytes 71119040 | solution.py:133
  136.5 4.5 %reshape.312 = f32[16,128,254]{2,1,0:T(8,128)} reshape(f32[16,32512]{1,0:T(8,128)S(1)} %slice.183) | data formatting | bytes 4161536 | tf_op jit(solution)/shard_map/while/body/eval_jaxpr/reshape | solution.py:27
  152.6 4.8 %reshape.313 = f32[16,128,255]{2,1,0:T(8,128)S(1)} reshape(f32[16,32640]{1,0:T(8,128)} %slice.185) | data formatting | bytes 4177920 | tf_op jit(solution)/shard_map/while/body/eval_jaxpr/reshape | solution.py:18
  171.4 4.5 %reshape.312 = f32[16,128,254]{2,1,0:T(8,128)} reshape(f32[16,32512]{1,0:T(8,128)S(1)} %slice.183) | data formatting | bytes 4161536 | tf_op jit(solution)/shard_map/while/body/eval_jaxpr/reshape | solution.py:27
  187.6 4.8 %reshape.313 = f32[16,128,255]{2,1,0:T(8,128)S(1)} reshape(f32[16,32640]{1,0:T(8,128)} %slice.185) | data formatting | bytes 4177920 | tf_op jit(solution)/shard_map/while/body/eval_jaxpr/reshape | solution.py:18
  206.4 4.5 %reshape.312 = f32[16,128,254]{2,1,0:T(8,128)} reshape(f32[16,32512]{1,0:T(8,128)S(1)} %slice.183) | data formatting | bytes 4161536 | tf_op jit(solution)/shard_map/while/body/eval_jaxpr/reshape | solution.py:27
  222.5 4.8 %reshape.313 = f32[16,128,255]{2,1,0:T(8,128)S(1)} reshape(f32[16,32640]{1,0:T(8,128)} %slice.185) | data formatting | bytes 4177920 | tf_op jit(solution)/shard_map/while/body/eval_jaxpr/reshape | solution.py:18
  233.4 5.8 %collective-permute-start.4 = (f32[16,128]{1,0:T(8,128)S(1)}, f32[16,128]{1,0:T(8,128)S(1)}, u32[]{:S(2)}, u32[]{:S(2)}) collective-permute-start(f32[16,128]{1,0:T(8,128)S(1)} %get-tuple-element.814), channel_id=1, source_target_pairs={{0,2},{2,0},{4,6},{6,4},{8,10},{10,8},{12,14},{14,12},{16,18},{18,... | collective-permute-start | bytes 24584 | tf_op jit(solution)/shard_map/ppermute | solution.py:139
  240.8 3.5 %collective-permute-start.5 = (f32[16,128]{1,0:T(8,128)S(1)}, f32[16,128]{1,0:T(8,128)S(1)}, u32[]{:S(2)}, u32[]{:S(2)}) collective-permute-start(f32[16,128]{1,0:T(8,128)S(1)} %add.208), channel_id=1, source_target_pairs={{0,4},{2,6},{4,0},{6,2},{8,12},{10,14},{12,8},{14,10},{16,20},{18,... | collective-permute-start | bytes 24584 | tf_op jit(solution)/shard_map/ppermute | solution.py:139
  245.9 6.4 %collective-permute-start.6 = (f32[16,128]{1,0:T(8,128)S(1)}, f32[16,128]{1,0:T(8,128)S(1)}, u32[]{:S(2)}, u32[]{:S(2)}) collective-permute-start(f32[16,128]{1,0:T(8,128)S(1)} %add.209), channel_id=1, source_target_pairs={{0,8},{2,10},{4,12},{6,14},{8,0},{10,2},{12,4},{14,6},{16,24},{18,... | collective-permute-start | bytes 24584 | tf_op jit(solution)/shard_map/ppermute | solution.py:139
  253.9 4.4 %collective-permute-start.7 = (f32[16,128]{1,0:T(8,128)S(1)}, f32[16,128]{1,0:T(8,128)S(1)}, u32[]{:S(2)}, u32[]{:S(2)}) collective-permute-start(f32[16,128]{1,0:T(8,128)S(1)} %add.210), channel_id=1, source_target_pairs={{0,16},{2,18},{4,20},{6,22},{8,24},{10,26},{12,28},{14,30},{16,0},... | collective-permute-start | bytes 24584 | tf_op jit(solution)/shard_map/ppermute | solution.py:139
  (266 shorter events, 162.2 us)
Async XLA Ops:
  17.0 4.4 %copy-start.10 = (s32[1,4]{1,0:T(1,128)S(1)}, s32[1,4]{1,0:T(1,128)}, u32[]{:S(2)}) copy-start(s32[1,4]{1,0:T(1,128)} %param.21) | copy-start | bytes 52
  19.4 4.4 %copy-start.8 = (s32[1,4,256]{2,1,0:T(4,128)S(1)}, s32[1,4,256]{2,1,0:T(4,128)}, u32[]{:S(2)}) copy-start(s32[1,4,256]{2,1,0:T(4,128)} %param.20) | copy-start | bytes 12292
  19.4 4.4 %copy-start.9 = (f32[16,128]{1,0:T(8,128)S(1)}, f32[16,128]{1,0:T(8,128)}, u32[]{:S(2)}) copy-start(f32[16,128]{1,0:T(8,128)} %param.19) | copy-start | bytes 24580
  23.8 21.0 %collective-permute-start = (bf16[128,1024]{0,1:T(8,128)(2,1)S(1)}, bf16[128,1024]{0,1:T(8,128)(2,1)S(1)}, u32[]{:S(2)}, u32[]{:S(2)}) collective-permute-start(bf16[128,1024]{0,1:T(8,128)(2,1)S(1)} %get-tuple-element.1186), channel_id=1, source_target_pairs={{0,2},{2,4},{4,6},{6,8},{8,10},{10,12},{12,14},{14,16},{16,18},{18... | collective-permute-start | bytes 786440 | tf_op jit(solution)/shard_map/while/body/eval_jaxpr/ppermute | solution.py:10
  28.7 16.8 %collective-permute-start.1 = (bf16[128,1024]{0,1:T(8,128)(2,1)}, bf16[128,1024]{0,1:T(8,128)(2,1)S(1)}, u32[]{:S(2)}, u32[]{:S(2)}) collective-permute-start(bf16[128,1024]{0,1:T(8,128)(2,1)} %get-tuple-element.1187), channel_id=1, source_target_pairs={{0,2},{2,4},{4,6},{6,8},{8,10},{10,12},{12,14},{14,16},{16,18},{18... | collective-permute-start | bytes 786440 | tf_op jit(solution)/shard_map/while/body/eval_jaxpr/ppermute | solution.py:10
  49.1 19.5 %collective-permute-start = (bf16[128,1024]{0,1:T(8,128)(2,1)S(1)}, bf16[128,1024]{0,1:T(8,128)(2,1)S(1)}, u32[]{:S(2)}, u32[]{:S(2)}) collective-permute-start(bf16[128,1024]{0,1:T(8,128)(2,1)S(1)} %get-tuple-element.1186), channel_id=1, source_target_pairs={{0,2},{2,4},{4,6},{6,8},{8,10},{10,12},{12,14},{14,16},{16,18},{18... | collective-permute-start | bytes 786440 | tf_op jit(solution)/shard_map/while/body/eval_jaxpr/ppermute | solution.py:10
  52.5 16.7 %collective-permute-start.1 = (bf16[128,1024]{0,1:T(8,128)(2,1)}, bf16[128,1024]{0,1:T(8,128)(2,1)S(1)}, u32[]{:S(2)}, u32[]{:S(2)}) collective-permute-start(bf16[128,1024]{0,1:T(8,128)(2,1)} %get-tuple-element.1187), channel_id=1, source_target_pairs={{0,2},{2,4},{4,6},{6,8},{8,10},{10,12},{12,14},{14,16},{16,18},{18... | collective-permute-start | bytes 786440 | tf_op jit(solution)/shard_map/while/body/eval_jaxpr/ppermute | solution.py:10
  72.8 19.5 %collective-permute-start = (bf16[128,1024]{0,1:T(8,128)(2,1)S(1)}, bf16[128,1024]{0,1:T(8,128)(2,1)S(1)}, u32[]{:S(2)}, u32[]{:S(2)}) collective-permute-start(bf16[128,1024]{0,1:T(8,128)(2,1)S(1)} %get-tuple-element.1186), channel_id=1, source_target_pairs={{0,2},{2,4},{4,6},{6,8},{8,10},{10,12},{12,14},{14,16},{16,18},{18... | collective-permute-start | bytes 786440 | tf_op jit(solution)/shard_map/while/body/eval_jaxpr/ppermute | solution.py:10
  76.2 16.7 %collective-permute-start.1 = (bf16[128,1024]{0,1:T(8,128)(2,1)}, bf16[128,1024]{0,1:T(8,128)(2,1)S(1)}, u32[]{:S(2)}, u32[]{:S(2)}) collective-permute-start(bf16[128,1024]{0,1:T(8,128)(2,1)} %get-tuple-element.1187), channel_id=1, source_target_pairs={{0,2},{2,4},{4,6},{6,8},{8,10},{10,12},{12,14},{14,16},{16,18},{18... | collective-permute-start | bytes 786440 | tf_op jit(solution)/shard_map/while/body/eval_jaxpr/ppermute | solution.py:10
  112.1 2.8 %copy-start.4 = (bf16[1,128,1024]{1,2,0:T(8,128)(2,1)S(1)}, bf16[1,128,1024]{1,2,0:T(8,128)(2,1)}, u32[]{:S(2)}) copy-start(bf16[1,128,1024]{1,2,0:T(8,128)(2,1)} %slice.141) | copy-start | bytes 786436
  128.5 31.0 %collective-permute-start.2 = (f32[128,1024]{0,1:T(8,128)}, f32[128,1024]{0,1:T(8,128)}, u32[]{:S(2)}, u32[]{:S(2)}) collective-permute-start(f32[128,1024]{0,1:T(8,128)} %get-tuple-element.1244), channel_id=1, source_target_pairs={{2,0},{4,2},{6,4},{8,6},{10,8},{12,10},{14,12},{16,14},{18,16},{20... | collective-permute-start | bytes 1572872 | tf_op jit(solution)/shard_map/while/body/eval_jaxpr/ppermute | solution.py:10
  129.8 31.8 %collective-permute-start.3 = (f32[128,1024]{0,1:T(8,128)}, f32[128,1024]{0,1:T(8,128)}, u32[]{:S(2)}, u32[]{:S(2)}) collective-permute-start(f32[128,1024]{0,1:T(8,128)} %get-tuple-element.1245), channel_id=1, source_target_pairs={{2,0},{4,2},{6,4},{8,6},{10,8},{12,10},{14,12},{16,14},{18,16},{20... | collective-permute-start | bytes 1572872 | tf_op jit(solution)/shard_map/while/body/eval_jaxpr/ppermute | solution.py:10
  157.6 1.9 copy-start
  159.5 4.0 %copy-start.3 = (f32[128,1024]{0,1:T(8,128)}, f32[128,1024]{0,1:T(8,128)S(1)}, u32[]{:S(2)}) copy-start(f32[128,1024]{0,1:T(8,128)S(1)} %bitcast_add_fusion.6) | copy-start | bytes 1572868 | tf_op jit(solution)/shard_map/while
  163.5 31.0 %collective-permute-start.2 = (f32[128,1024]{0,1:T(8,128)}, f32[128,1024]{0,1:T(8,128)}, u32[]{:S(2)}, u32[]{:S(2)}) collective-permute-start(f32[128,1024]{0,1:T(8,128)} %get-tuple-element.1244), channel_id=1, source_target_pairs={{2,0},{4,2},{6,4},{8,6},{10,8},{12,10},{14,12},{16,14},{18,16},{20... | collective-permute-start | bytes 1572872 | tf_op jit(solution)/shard_map/while/body/eval_jaxpr/ppermute | solution.py:10
  164.8 31.8 %collective-permute-start.3 = (f32[128,1024]{0,1:T(8,128)}, f32[128,1024]{0,1:T(8,128)}, u32[]{:S(2)}, u32[]{:S(2)}) collective-permute-start(f32[128,1024]{0,1:T(8,128)} %get-tuple-element.1245), channel_id=1, source_target_pairs={{2,0},{4,2},{6,4},{8,6},{10,8},{12,10},{14,12},{16,14},{18,16},{20... | collective-permute-start | bytes 1572872 | tf_op jit(solution)/shard_map/while/body/eval_jaxpr/ppermute | solution.py:10
  194.5 4.0 %copy-start.3 = (f32[128,1024]{0,1:T(8,128)}, f32[128,1024]{0,1:T(8,128)S(1)}, u32[]{:S(2)}) copy-start(f32[128,1024]{0,1:T(8,128)S(1)} %bitcast_add_fusion.6) | copy-start | bytes 1572868 | tf_op jit(solution)/shard_map/while
  198.5 31.0 %collective-permute-start.2 = (f32[128,1024]{0,1:T(8,128)}, f32[128,1024]{0,1:T(8,128)}, u32[]{:S(2)}, u32[]{:S(2)}) collective-permute-start(f32[128,1024]{0,1:T(8,128)} %get-tuple-element.1244), channel_id=1, source_target_pairs={{2,0},{4,2},{6,4},{8,6},{10,8},{12,10},{14,12},{16,14},{18,16},{20... | collective-permute-start | bytes 1572872 | tf_op jit(solution)/shard_map/while/body/eval_jaxpr/ppermute | solution.py:10
  199.7 31.8 %collective-permute-start.3 = (f32[128,1024]{0,1:T(8,128)}, f32[128,1024]{0,1:T(8,128)}, u32[]{:S(2)}, u32[]{:S(2)}) collective-permute-start(f32[128,1024]{0,1:T(8,128)} %get-tuple-element.1245), channel_id=1, source_target_pairs={{2,0},{4,2},{6,4},{8,6},{10,8},{12,10},{14,12},{16,14},{18,16},{20... | collective-permute-start | bytes 1572872 | tf_op jit(solution)/shard_map/while/body/eval_jaxpr/ppermute | solution.py:10
  229.4 4.0 %copy-start.3 = (f32[128,1024]{0,1:T(8,128)}, f32[128,1024]{0,1:T(8,128)S(1)}, u32[]{:S(2)}) copy-start(f32[128,1024]{0,1:T(8,128)S(1)} %bitcast_add_fusion.6) | copy-start | bytes 1572868 | tf_op jit(solution)/shard_map/while
  233.4 7.4 %collective-permute-start.4 = (f32[16,128]{1,0:T(8,128)S(1)}, f32[16,128]{1,0:T(8,128)S(1)}, u32[]{:S(2)}, u32[]{:S(2)}) collective-permute-start(f32[16,128]{1,0:T(8,128)S(1)} %get-tuple-element.814), channel_id=1, source_target_pairs={{0,2},{2,0},{4,6},{6,4},{8,10},{10,8},{12,14},{14,12},{16,18},{18,... | collective-permute-start | bytes 24584 | tf_op jit(solution)/shard_map/ppermute | solution.py:139
  240.8 5.1 %collective-permute-start.5 = (f32[16,128]{1,0:T(8,128)S(1)}, f32[16,128]{1,0:T(8,128)S(1)}, u32[]{:S(2)}, u32[]{:S(2)}) collective-permute-start(f32[16,128]{1,0:T(8,128)S(1)} %add.208), channel_id=1, source_target_pairs={{0,4},{2,6},{4,0},{6,2},{8,12},{10,14},{12,8},{14,10},{16,20},{18,... | collective-permute-start | bytes 24584 | tf_op jit(solution)/shard_map/ppermute | solution.py:139
  245.9 8.0 %collective-permute-start.6 = (f32[16,128]{1,0:T(8,128)S(1)}, f32[16,128]{1,0:T(8,128)S(1)}, u32[]{:S(2)}, u32[]{:S(2)}) collective-permute-start(f32[16,128]{1,0:T(8,128)S(1)} %add.209), channel_id=1, source_target_pairs={{0,8},{2,10},{4,12},{6,14},{8,0},{10,2},{12,4},{14,6},{16,24},{18,... | collective-permute-start | bytes 24584 | tf_op jit(solution)/shard_map/ppermute | solution.py:139
  253.9 10.1 %collective-permute-start.7 = (f32[16,128]{1,0:T(8,128)S(1)}, f32[16,128]{1,0:T(8,128)S(1)}, u32[]{:S(2)}, u32[]{:S(2)}) collective-permute-start(f32[16,128]{1,0:T(8,128)S(1)} %add.210), channel_id=1, source_target_pairs={{0,16},{2,18},{4,20},{6,22},{8,24},{10,26},{12,28},{14,30},{16,0},... | collective-permute-start | bytes 24584 | tf_op jit(solution)/shard_map/ppermute | solution.py:139
  (19 other events, 28.4 us)
